TPU v7x, 32 devices: a whole 2x2x4 slice. The times are simulated.
32 devices in a mesh: parts: 2 (over y), row: 16 (over z, x, core).
Axes of the slice: x: 2, y: 2, z: 4, core: 2. Of those that a mesh axis runs over, the one named last changes fastest.
Arguments:
- traces: bfloat16 [256, 2, 12000], P(('parts', 'row')), parts along dimension 0, may hold values from -160 to 160
- valid_mask: int32 [256, 2], P(('parts', 'row')), parts along dimension 0, may hold values 0 or 1
- pair_table: int32 [32, 10], P(('parts', 'row')), parts along dimension 0, may hold values from 0 to 15, as said below
- stack_in: float32 [32, 10, 8, 8, 401], P(('parts', 'row')), parts along dimension 0, may hold values from -6 to 6
Outputs:
- stacks: float32 [32, 10, 8, 8, 401], P(('parts', 'row')), parts along dimension 0
There are 2 independent parts, one for each index of `parts`. A program takes and returns all parts, laid end to end along the dimension named above; each array names one. Nothing has to cross between parts.
Inputs may be any that keep to these rules, and one draw needn't show every extreme that they name: `pair_table`: row i lists the panels (i + k) mod 16 for k = -1 to 8, each once, in an order that varies from row to row.
All inputs are finite; a program needn't handle non-finite values. No bound on the sum of `valid_mask` on one device may be relied on, other than what follows from the above.
Results may differ from a plain program's by a relative error of at most 0.0032.
Values may be sent and summed in bfloat16 or wider, within the bound.
No kernel may reach another device: no remote copies, remote signals or barrier semaphores. Data moves between devices by JAX's collectives and lax.ppermute only.
A program may use at most 128 MiB of HBM per device.

v0:
```python
import math
import jax
import jax.numpy as jnp
from jax import lax
from jax.sharding import PartitionSpec as P

SAMPLES = 12000
FLO = 6
BINS = 595
HALF = 40
LAGS = 401
epsilon = 1e-06


def spectra_of(rows, samples, first_bin, bins):
    length = samples // 8
    freq = first_bin + jnp.arange(bins, dtype=jnp.int32)

    def absorb(totals, block_index):
        first_row = block_index * length
        segment = lax.dynamic_slice_in_dim(rows, first_row, length, 1)
        times = first_row + jnp.arange(length, dtype=jnp.int32)
        angle = (times[:, None] * freq[None, :] % samples).astype(jnp.float32) * (
            2.0 * math.pi / samples
        )
        table = jnp.concatenate([jnp.cos(angle), -jnp.sin(angle)], axis=1).astype(jnp.bfloat16)
        return (totals + jnp.dot(segment, table, preferred_element_type=jnp.float32), None)

    start_total = jnp.zeros((rows.shape[0], 2 * bins), jnp.float32)
    totals, unused = lax.scan(absorb, start_total, jnp.arange(8, dtype=jnp.int32))
    return totals


def whiten_rows(traces, valid_mask, first_bin, bins, half_width):
    chans, minutes, samples = traces.shape
    spectrum = spectra_of(traces.reshape(chans * minutes, samples), samples, first_bin, bins)
    real_part = spectrum[:, :bins]
    imag_part = spectrum[:, bins:]
    power = real_part * real_part + imag_part * imag_part
    positions = jnp.arange(bins, dtype=jnp.int32)
    near = (jnp.abs(positions[:, None] - positions[None, :]) <= half_width).astype(jnp.float32)
    window = near / jnp.sum(near, axis=0, keepdims=True)
    smooth = jnp.dot(power, window, precision=lax.Precision.HIGHEST)
    divisor = jnp.sqrt(smooth + epsilon)
    flags = valid_mask.reshape(-1, 1).astype(jnp.float32)
    whitened = spectrum * flags / jnp.concatenate([divisor, divisor], axis=1)
    return whitened.astype(jnp.bfloat16).reshape(chans, minutes, 2 * bins)


def lag_matrix(first_bin, bins, lags, samples):
    freq = first_bin + jnp.arange(bins, dtype=jnp.int32)
    shifts = jnp.arange(lags, dtype=jnp.int32) - (lags - 1) // 2
    angle = (freq[:, None] * shifts[None, :] % samples).astype(jnp.float32) * (
        2.0 * math.pi / samples
    )
    return jnp.concatenate([jnp.cos(angle), -jnp.sin(angle)], axis=0).astype(jnp.bfloat16)


def tile_corr(own_white, own_flags, partner_white, partner_flags, lag_table):
    bins = lag_table.shape[0] // 2
    own = own_white.astype(jnp.float32)
    partner = partner_white.astype(jnp.float32)
    shape = (partner.shape[0], own.shape[0], partner.shape[1], bins)
    real_sum = jnp.zeros(shape, jnp.float32)
    imag_sum = jnp.zeros(shape, jnp.float32)
    joint_sum = jnp.zeros(shape[:3], jnp.float32)
    for minute in range(own.shape[1]):
        own_real = own[:, minute, :bins][None, :, None, :]
        own_imag = own[:, minute, bins:][None, :, None, :]
        part_real = partner[:, :, minute, :bins][:, None, :, :]
        part_imag = partner[:, :, minute, bins:][:, None, :, :]
        real_sum = real_sum + (own_real * part_real + own_imag * part_imag)
        imag_sum = imag_sum + (own_imag * part_real - own_real * part_imag)
        own_valid = own_flags[:, minute].astype(jnp.float32)[None, :, None]
        part_valid = partner_flags[:, :, minute].astype(jnp.float32)[:, None, :]
        joint_sum = joint_sum + own_valid * part_valid
    inverse = 1.0 / jnp.maximum(joint_sum, 1.0)
    cross = (jnp.concatenate([real_sum, imag_sum], axis=-1) * inverse[..., None]).astype(
        jnp.bfloat16
    )
    corr = jnp.dot(cross.reshape(-1, 2 * bins), lag_table, preferred_element_type=jnp.float32) * (
        1.0 / math.sqrt(bins)
    )
    return corr.reshape(shape[0], shape[1], shape[2], lag_table.shape[1])


def shards(traces, valid_mask, pair_table, stack_in):
    panel_count = lax.axis_size("row")
    chans = traces.shape[0]
    minutes = traces.shape[1]
    whitened = whiten_rows(traces, valid_mask, FLO, BINS, HALF)
    own_flags = valid_mask.astype(jnp.bfloat16)
    lag_table = lag_matrix(FLO, BINS, LAGS, SAMPLES)
    table_row = pair_table[0]
    base_stack = stack_in[0]
    whole_white, whole_flags = (
        lax.all_gather(whitened, "row", axis=0, tiled=True),
        lax.all_gather(own_flags, "row", axis=0, tiled=True),
    )
    panels = whole_white.reshape(panel_count, chans, minutes, whitened.shape[2])
    panel_flags = whole_flags.reshape(panel_count, chans, minutes)
    partner = jnp.take(panels, table_row, axis=0)
    partner_flags = jnp.take(panel_flags, table_row, axis=0)
    result = base_stack + tile_corr(whitened, own_flags, partner, partner_flags, lag_table)
    return result[None]


def solution(mesh):
    in_specs = (
        P(("parts", "row"), None, None),
        P(("parts", "row"), None),
        P(("parts", "row"), None),
        P(("parts", "row"), None, None, None, None),
    )
    out_specs = P(("parts", "row"), None, None, None, None)
    return jax.shard_map(shards, mesh=mesh, in_specs=in_specs, out_specs=out_specs, check_vma=False)
```

profile of v0, /device:TPU:0, one launch (start us, length us, event | category | flops | bytes accessed | tf_op | source)
XLA Modules:
  0.0 214.5 jit_solution(12585721607296174629)
XLA Ops:
  0.0 0.7 compare_and_fusion
  0.7 0.7 fusion.46
  1.3 0.8 fusion.52
  2.1 0.1 copy.33
  2.2 0.1 convert_element_type.89
  2.3 0.1 convert_reduce_fusion
  2.4 23.0 %all-gather = bf16[16,8,2]{1,2,0:T(2,128)(2,1)S(1)} all-gather(bf16[1,8,2]{1,2,0:T(2,128)(2,1)S(1)} %bitcast.50), channel_id=1, replica_groups=mesh['parts'=2,'row'=16] {'row'}, dimensions={0}, use_global_device_ids=true | all-gather | bytes 544 | tf_op jit(solution)/shard_map/all_gather | solution.py:98
  25.4 0.6 gather_fusion.1
  25.9 0.1 copy.34
  26.1 0.1 copy.35
  26.1 0.1 copy.36
  26.2 0.1 maximum_divide_fusion.1
  26.3 0.1 div.25
  26.4 1.3 reshape.162
  27.7 151.3 %while.13 = (s32[]{:T(128)}, f32[16,1190]{1,0:T(8,128)S(1)}, s32[8]{0:T(128)S(1)}, bf16[16,12000]{1,0:T(8,128)(2,1)S(1)}, s32[]{:T(128)}, /*index=5*/s32[1]{0:T(128)}, s32[]{:T(128)}, s32[]{:T(128)}) while((s32[]{:T(128)}, f32[16,1190]{1,0:T(8,128)S(1)}, s32[8]{0:T(128)S(1)}, bf16[16,12000]{1,0:T(8,128)(2,1)S(1)}, s32[]{:T(128)}, ...), condition=%wide.region_1.2_spmd.clone, body=%wide.region_0.1_spmd.clone.sunk | while | flops 75010184 | bytes 7644401 | solution.py:30
  27.7 0.7 dynamic_slice.20
  29.0 16.6 %cosine_convert_fusion.3 = (bf16[1500,595]{1,0:T(8,128)(2,1)S(1)}, bf16[1500,595]{1,0:T(8,128)(2,1)S(1)}) fusion(s32[595]{0:T(1024)S(1)} %iota_add_fusion.6, s32[1500]{0:T(1024)S(1)} %iota_add_fusion.7), kind=kLoop, calls=%fused_computation.11.clone.1 | loop fusion | flops 10710000 | bytes 3578380 | tf_op jit(solution)/shard_map/convert
  45.6 1.0 fusion.58
  46.6 0.6 dynamic_slice.20
  47.9 16.6 %cosine_convert_fusion.3 = (bf16[1500,595]{1,0:T(8,128)(2,1)S(1)}, bf16[1500,595]{1,0:T(8,128)(2,1)S(1)}) fusion(s32[595]{0:T(1024)S(1)} %iota_add_fusion.6, s32[1500]{0:T(1024)S(1)} %iota_add_fusion.7), kind=kLoop, calls=%fused_computation.11.clone.1 | loop fusion | flops 10710000 | bytes 3578380 | tf_op jit(solution)/shard_map/convert
  64.5 1.0 fusion.58
  65.5 0.6 dynamic_slice.20
  66.8 16.6 %cosine_convert_fusion.3 = (bf16[1500,595]{1,0:T(8,128)(2,1)S(1)}, bf16[1500,595]{1,0:T(8,128)(2,1)S(1)}) fusion(s32[595]{0:T(1024)S(1)} %iota_add_fusion.6, s32[1500]{0:T(1024)S(1)} %iota_add_fusion.7), kind=kLoop, calls=%fused_computation.11.clone.1 | loop fusion | flops 10710000 | bytes 3578380 | tf_op jit(solution)/shard_map/convert
  83.4 1.0 fusion.58
  84.4 0.6 dynamic_slice.20
  85.7 16.6 %cosine_convert_fusion.3 = (bf16[1500,595]{1,0:T(8,128)(2,1)S(1)}, bf16[1500,595]{1,0:T(8,128)(2,1)S(1)}) fusion(s32[595]{0:T(1024)S(1)} %iota_add_fusion.6, s32[1500]{0:T(1024)S(1)} %iota_add_fusion.7), kind=kLoop, calls=%fused_computation.11.clone.1 | loop fusion | flops 10710000 | bytes 3578380 | tf_op jit(solution)/shard_map/convert
  102.3 1.0 fusion.58
  103.3 0.6 dynamic_slice.20
  104.6 16.6 %cosine_convert_fusion.3 = (bf16[1500,595]{1,0:T(8,128)(2,1)S(1)}, bf16[1500,595]{1,0:T(8,128)(2,1)S(1)}) fusion(s32[595]{0:T(1024)S(1)} %iota_add_fusion.6, s32[1500]{0:T(1024)S(1)} %iota_add_fusion.7), kind=kLoop, calls=%fused_computation.11.clone.1 | loop fusion | flops 10710000 | bytes 3578380 | tf_op jit(solution)/shard_map/convert
  121.2 1.0 fusion.58
  122.2 0.6 dynamic_slice.20
  123.5 16.6 %cosine_convert_fusion.3 = (bf16[1500,595]{1,0:T(8,128)(2,1)S(1)}, bf16[1500,595]{1,0:T(8,128)(2,1)S(1)}) fusion(s32[595]{0:T(1024)S(1)} %iota_add_fusion.6, s32[1500]{0:T(1024)S(1)} %iota_add_fusion.7), kind=kLoop, calls=%fused_computation.11.clone.1 | loop fusion | flops 10710000 | bytes 3578380 | tf_op jit(solution)/shard_map/convert
  140.1 1.0 fusion.58
  141.1 0.6 dynamic_slice.20
  142.4 16.6 %cosine_convert_fusion.3 = (bf16[1500,595]{1,0:T(8,128)(2,1)S(1)}, bf16[1500,595]{1,0:T(8,128)(2,1)S(1)}) fusion(s32[595]{0:T(1024)S(1)} %iota_add_fusion.6, s32[1500]{0:T(1024)S(1)} %iota_add_fusion.7), kind=kLoop, calls=%fused_computation.11.clone.1 | loop fusion | flops 10710000 | bytes 3578380 | tf_op jit(solution)/shard_map/convert
  159.0 1.0 fusion.58
  160.0 0.6 dynamic_slice.20
  161.4 16.6 %cosine_convert_fusion.3 = (bf16[1500,595]{1,0:T(8,128)(2,1)S(1)}, bf16[1500,595]{1,0:T(8,128)(2,1)S(1)}) fusion(s32[595]{0:T(1024)S(1)} %iota_add_fusion.6, s32[1500]{0:T(1024)S(1)} %iota_add_fusion.7), kind=kLoop, calls=%fused_computation.11.clone.1 | loop fusion | flops 10710000 | bytes 3578380 | tf_op jit(solution)/shard_map/convert
  177.9 1.0 fusion.58
  179.0 0.8 fusion.34
  179.8 0.1 fusion.38
  179.9 0.1 fusion.51
  180.1 19.4 %all_gather.6 = bf16[128,2,1190]{2,1,0:T(2,128)(2,1)S(1)} all-gather(bf16[8,2,1190]{2,1,0:T(2,128)(2,1)S(1)} %reshape.163), channel_id=1, replica_groups=mesh['parts'=2,'row'=16] {'row'}, dimensions={0}, use_global_device_ids=true | all-gather | bytes 647360 | tf_op jit(solution)/shard_map/all_gather | solution.py:97
  199.4 1.4 gather_fusion
  200.9 0.4 fusion.37
  201.3 1.2 fusion.50
  202.6 5.6 %cosine_convert_fusion.1 = (bf16[595,401]{1,0:T(8,128)(2,1)S(1)}, bf16[595,401]{1,0:T(8,128)(2,1)S(1)}) fusion(s32[401]{0:T(512)S(1)} %iota_add_fusion.3, s32[595]{0:T(1024)S(1)} %iota_add_fusion.2), kind=kLoop, calls=%fused_computation.37 | loop fusion | flops 2863140 | bytes 958364 | tf_op jit(solution)/shard_map/convert.6
  208.1 0.8 add_add_fusion
  208.9 2.4 %fusion.22 = f32[640,401]{0,1:T(8,128)} fusion(f32[640,595]{1,0:T(8,128)S(1)} %bitcast.49, f32[640,595]{1,0:T(8,128)S(1)} %bitcast.48, f32[640]{0:T(1024)S(1)} %div.25, bf16[595,401]{1,0:T(8,128)(2,1)S(1)} %get-tuple-element.110, bf16[595,401]{1,0:T(8,128)(2,1)S(1)} %get-tuple-element.109), kind=kOutput, calls=%fused_computation.33 | convolution fusion | flops 615253376 | bytes 5029900 | tf_op jit(solution)/shard_map/dot_general | solution.py:81
  211.3 0.0 copy-start
  211.3 1.7 copy.37
  213.0 0.0 copy-done
  213.1 1.4 add.141
  (29 shorter events, 0.2 us)
Async XLA Ops:
  211.3 1.7 copy-start
where the time goes:
time: 215 us; the launch traced here: 214 us
  other arithmetic  143 us (67%)
  blocking collectives  42.3 us (20%)
  local copies, waits for them, and re-layouts  12.1 us (6%)
  matrix products  11.3 us (5%)
  loops' own time  5.26 us (2%)
    another operation x9, other arithmetic  138 us
    all_gather x1, blocking collectives, shards(): lax.all_gather(own_flags, 'row', axis=0, tiled=True)  23 us
    all_gather x1, blocking collectives, shards(): lax.all_gather(whitened, 'row', axis=0, tiled=True)  19.4 us
    dot_general x8, matrix products, absorb(): jnp.dot(segment, table, preferred_element_type=jnp.float32)  8.12 us
    another operation x1, loops' own time, spectra_of(): lax.scan(absorb, start_total, jnp.arange(8, dtype=jnp.int32))  5.26 us
    dynamic_slice x8, local copies, waits for them, and re-layouts, spectra_of(): lax.scan(absorb, start_total, jnp.arange(8, dtype=jnp.int32))  5.19 us

commit v1 on v0

--- a/solution.py
+++ b/solution.py
@@ -10,6 +10,19 @@
 HALF = 40
 LAGS = 401
 epsilon = 1e-06
+
+
+def gather_around(shard, axis, dim):
+    ways = lax.axis_size(axis)
+    up = [(d, (d + 1) % ways) for d in range(ways)]
+    down = [(d, (d - 1) % ways) for d in range(ways)]
+    earlier, later = ([shard], [shard])
+    for _ in range(ways // 2):
+        earlier.append(lax.ppermute(earlier[-1], axis, up))
+    for _ in range((ways - 1) // 2):
+        later.append(lax.ppermute(later[-1], axis, down))
+    line = jnp.concatenate([*earlier[::-1], *later[1:]], axis=dim)
+    return jnp.roll(line, (lax.axis_index(axis) - ways // 2) * shard.shape[dim], axis=dim)
 
 
 def spectra_of(rows, samples, first_bin, bins):
@@ -95,7 +108,7 @@
     base_stack = stack_in[0]
     whole_white, whole_flags = (
         lax.all_gather(whitened, "row", axis=0, tiled=True),
-        lax.all_gather(own_flags, "row", axis=0, tiled=True),
+        gather_around(own_flags, "row", 0),
     )
     panels = whole_white.reshape(panel_count, chans, minutes, whitened.shape[2])
     panel_flags = whole_flags.reshape(panel_count, chans, minutes)

time: 215 us -> 240 us (1.12)
  starting transfers between devices: 0 us -> 28 us
  blocking collectives: 42.3 us -> 20.5 us
  waiting for transfers between devices: 0 us -> 17.8 us
    ppermute x0 -> x15, starting transfers between devices: none -> 28 us  [the longest x7 28 us: gather_around(): later.append(lax.ppermute(later[-1], axis, down))]
    all_gather x1 -> x0, blocking collectives: 23 us -> none  [shards(): lax.all_gather(own_flags, 'row', axis=0, tiled=True)]
    ppermute x0 -> x15, waiting for transfers between devices: none -> 17.8 us  [the longest x8 11.3 us: gather_around(): earlier.append(lax.ppermute(earlier[-1], axis, up))]
  transfers between devices with their start and end apart: 0 -> 15, of which waited for: 0 -> 7; matrix products, arithmetic and copies ran while one was open for 0% -> 67% of each run, Pallas kernels for 0% -> 0%
where the time goes in v1:
time: 240 us
  other arithmetic  144 us (60%)
  starting transfers between devices  28 us (12%)
  blocking collectives  20.5 us (9%)
  waiting for transfers between devices  17.8 us (7%)
  matrix products  12.5 us (5%)
  local copies, waits for them, and re-layouts  11.9 us (5%)
  loops' own time  4.85 us (2%)
    another operation x9, other arithmetic  139 us
    ppermute x7, starting transfers between devices, gather_around(): later.append(lax.ppermute(later[-1], axis, down))  28 us
    all_gather x1, blocking collectives, shards(): lax.all_gather(whitened, 'row', axis=0, tiled=True)  20.5 us
    ppermute x8, waiting for transfers between devices, gather_around(): earlier.append(lax.ppermute(earlier[-1], axis, up))  11.3 us
    dot_general x8, matrix products, absorb(): jnp.dot(segment, table, preferred_element_type=jnp.float32)  8.12 us
    ppermute x7, waiting for transfers between devices, gather_around(): later.append(lax.ppermute(later[-1], axis, down))  6.45 us
    another operation x1, loops' own time, spectra_of(): lax.scan(absorb, start_total, jnp.arange(8, dtype=jnp.int32))  4.85 us
  transfers between devices with their start and end apart: 15, of which 7 were waited for; matrix products, arithmetic and copies ran while one was open for 67% of the time, Pallas kernels for 0%

profile of v1, /device:TPU:0, one launch (start us, length us, event | category | flops | bytes accessed | tf_op | source)
XLA Modules:
  0.0 239.8 jit_solution(4885862779120431734)
XLA Ops:
  0.0 0.8 fusion.52
  0.8 5.4 %collective-permute-start.8 = (bf16[8,2]{0,1:T(2,128)(2,1)S(1)}, bf16[8,2]{0,1:T(2,128)(2,1)S(1)}, u32[]{:S(2)}, u32[]{:S(2)}) collective-permute-start(bf16[8,2]{0,1:T(2,128)(2,1)S(1)} %get-tuple-element.113), channel_id=1, source_target_pairs={{0,15},{1,0},{2,1},{3,2},{4,3},{5,4},{6,5},{7,6},{8,7},{9,8},{10,9... | collective-permute-start | bytes 104 | tf_op jit(solution)/shard_map/ppermute | solution.py:23
  6.2 0.7 compare_and_fusion
  6.8 0.7 fusion.46
  7.5 0.1 convert_reduce_fusion
  7.8 1.3 reshape.162
  9.1 150.4 %while.13 = (s32[]{:T(128)}, f32[16,1190]{1,0:T(8,128)S(1)}, s32[8]{0:T(128)S(1)}, bf16[16,12000]{1,0:T(8,128)(2,1)S(1)}, s32[]{:T(128)}, /*index=5*/s32[1]{0:T(128)}, s32[]{:T(128)}, s32[]{:T(128)}) while((s32[]{:T(128)}, f32[16,1190]{1,0:T(8,128)S(1)}, s32[8]{0:T(128)S(1)}, bf16[16,12000]{1,0:T(8,128)(2,1)S(1)}, s32[]{:T(128)}, ...), condition=%wide.region_1.2_spmd.clone, body=%wide.region_0.1_spmd.clone.sunk | while | flops 75010184 | bytes 7644401 | solution.py:43
  9.1 0.6 dynamic_slice.26
  10.3 16.6 %cosine_convert_fusion.3 = (bf16[1500,595]{1,0:T(8,128)(2,1)S(1)}, bf16[1500,595]{1,0:T(8,128)(2,1)S(1)}) fusion(s32[595]{0:T(1024)S(1)} %iota_add_fusion.6, s32[1500]{0:T(1024)S(1)} %iota_add_fusion.7), kind=kLoop, calls=%fused_computation.11.clone.1 | loop fusion | flops 10710000 | bytes 3578380 | tf_op jit(solution)/shard_map/convert
  26.9 1.0 fusion.58
  27.9 0.6 dynamic_slice.26
  29.1 16.6 %cosine_convert_fusion.3 = (bf16[1500,595]{1,0:T(8,128)(2,1)S(1)}, bf16[1500,595]{1,0:T(8,128)(2,1)S(1)}) fusion(s32[595]{0:T(1024)S(1)} %iota_add_fusion.6, s32[1500]{0:T(1024)S(1)} %iota_add_fusion.7), kind=kLoop, calls=%fused_computation.11.clone.1 | loop fusion | flops 10710000 | bytes 3578380 | tf_op jit(solution)/shard_map/convert
  45.7 1.0 fusion.58
  46.7 0.6 dynamic_slice.26
  47.9 16.6 %cosine_convert_fusion.3 = (bf16[1500,595]{1,0:T(8,128)(2,1)S(1)}, bf16[1500,595]{1,0:T(8,128)(2,1)S(1)}) fusion(s32[595]{0:T(1024)S(1)} %iota_add_fusion.6, s32[1500]{0:T(1024)S(1)} %iota_add_fusion.7), kind=kLoop, calls=%fused_computation.11.clone.1 | loop fusion | flops 10710000 | bytes 3578380 | tf_op jit(solution)/shard_map/convert
  64.5 1.0 fusion.58
  65.5 0.6 dynamic_slice.26
  66.7 16.6 %cosine_convert_fusion.3 = (bf16[1500,595]{1,0:T(8,128)(2,1)S(1)}, bf16[1500,595]{1,0:T(8,128)(2,1)S(1)}) fusion(s32[595]{0:T(1024)S(1)} %iota_add_fusion.6, s32[1500]{0:T(1024)S(1)} %iota_add_fusion.7), kind=kLoop, calls=%fused_computation.11.clone.1 | loop fusion | flops 10710000 | bytes 3578380 | tf_op jit(solution)/shard_map/convert
  83.3 1.0 fusion.58
  84.3 0.6 dynamic_slice.26
  85.5 16.6 %cosine_convert_fusion.3 = (bf16[1500,595]{1,0:T(8,128)(2,1)S(1)}, bf16[1500,595]{1,0:T(8,128)(2,1)S(1)}) fusion(s32[595]{0:T(1024)S(1)} %iota_add_fusion.6, s32[1500]{0:T(1024)S(1)} %iota_add_fusion.7), kind=kLoop, calls=%fused_computation.11.clone.1 | loop fusion | flops 10710000 | bytes 3578380 | tf_op jit(solution)/shard_map/convert
  102.1 1.0 fusion.58
  103.1 0.6 dynamic_slice.26
  104.3 16.6 %cosine_convert_fusion.3 = (bf16[1500,595]{1,0:T(8,128)(2,1)S(1)}, bf16[1500,595]{1,0:T(8,128)(2,1)S(1)}) fusion(s32[595]{0:T(1024)S(1)} %iota_add_fusion.6, s32[1500]{0:T(1024)S(1)} %iota_add_fusion.7), kind=kLoop, calls=%fused_computation.11.clone.1 | loop fusion | flops 10710000 | bytes 3578380 | tf_op jit(solution)/shard_map/convert
  120.9 1.0 fusion.58
  121.9 0.6 dynamic_slice.26
  123.1 16.6 %cosine_convert_fusion.3 = (bf16[1500,595]{1,0:T(8,128)(2,1)S(1)}, bf16[1500,595]{1,0:T(8,128)(2,1)S(1)}) fusion(s32[595]{0:T(1024)S(1)} %iota_add_fusion.6, s32[1500]{0:T(1024)S(1)} %iota_add_fusion.7), kind=kLoop, calls=%fused_computation.11.clone.1 | loop fusion | flops 10710000 | bytes 3578380 | tf_op jit(solution)/shard_map/convert
  139.7 1.0 fusion.58
  140.7 0.6 dynamic_slice.26
  141.9 16.6 %cosine_convert_fusion.3 = (bf16[1500,595]{1,0:T(8,128)(2,1)S(1)}, bf16[1500,595]{1,0:T(8,128)(2,1)S(1)}) fusion(s32[595]{0:T(1024)S(1)} %iota_add_fusion.6, s32[1500]{0:T(1024)S(1)} %iota_add_fusion.7), kind=kLoop, calls=%fused_computation.11.clone.1 | loop fusion | flops 10710000 | bytes 3578380 | tf_op jit(solution)/shard_map/convert
  158.5 1.0 fusion.58
  159.5 0.8 fusion.34
  160.3 0.1 fusion.38
  160.4 0.1 fusion.51
  160.6 20.5 %all_gather.3 = bf16[128,2,1190]{2,1,0:T(2,128)(2,1)S(1)} all-gather(bf16[8,2,1190]{2,1,0:T(2,128)(2,1)S(1)} %reshape.163), channel_id=1, replica_groups=mesh['parts'=2,'row'=16] {'row'}, dimensions={0}, use_global_device_ids=true | all-gather | bytes 647360 | tf_op jit(solution)/shard_map/all_gather | solution.py:110
  181.0 1.4 gather_fusion
  182.4 0.4 fusion.37
  182.9 1.2 fusion.50
  184.2 6.3 %cosine_convert_fusion.1 = (bf16[595,401]{1,0:T(8,128)(2,1)}, bf16[595,401]{1,0:T(8,128)(2,1)}) fusion(s32[401]{0:T(512)S(1)} %iota_add_fusion.3, s32[595]{0:T(1024)S(1)} %iota_add_fusion.2), kind=kLoop, calls=%fused_computation.37 | loop fusion | flops 2863140 | bytes 958364 | tf_op jit(solution)/shard_map/convert.6
  190.5 0.8 add_add_fusion
  191.2 0.8 collective-permute-start.9
  192.0 1.3 collective-permute-done.9
  193.3 4.4 %collective-permute-start.10 = (bf16[8,2]{0,1:T(2,128)(2,1)S(1)}, bf16[8,2]{0,1:T(2,128)(2,1)S(1)}, u32[]{:S(2)}, u32[]{:S(2)}) collective-permute-start(bf16[8,2]{0,1:T(2,128)(2,1)S(1)} %collective-permute-done.9), channel_id=1, source_target_pairs={{0,15},{1,0},{2,1},{3,2},{4,3},{5,4},{6,5},{7,6},{8,7},{9,8},{10,9... | collective-permute-start | bytes 104 | tf_op jit(solution)/shard_map/ppermute | solution.py:23
  197.7 1.3 collective-permute-done.10
  199.0 4.4 %collective-permute-start.11 = (bf16[8,2]{0,1:T(2,128)(2,1)S(1)}, bf16[8,2]{0,1:T(2,128)(2,1)S(1)}, u32[]{:S(2)}, u32[]{:S(2)}) collective-permute-start(bf16[8,2]{0,1:T(2,128)(2,1)S(1)} %collective-permute-done.10), channel_id=1, source_target_pairs={{0,15},{1,0},{2,1},{3,2},{4,3},{5,4},{6,5},{7,6},{8,7},{9,8},{10,9... | collective-permute-start | bytes 104 | tf_op jit(solution)/shard_map/ppermute | solution.py:23
  203.3 1.3 collective-permute-done.11
  204.6 4.4 %collective-permute-start.12 = (bf16[8,2]{0,1:T(2,128)(2,1)S(1)}, bf16[8,2]{0,1:T(2,128)(2,1)S(1)}, u32[]{:S(2)}, u32[]{:S(2)}) collective-permute-start(bf16[8,2]{0,1:T(2,128)(2,1)S(1)} %collective-permute-done.11), channel_id=1, source_target_pairs={{0,15},{1,0},{2,1},{3,2},{4,3},{5,4},{6,5},{7,6},{8,7},{9,8},{10,9... | collective-permute-start | bytes 104 | tf_op jit(solution)/shard_map/ppermute | solution.py:23
  209.0 1.3 collective-permute-done.12
  210.3 4.4 %collective-permute-start.13 = (bf16[8,2]{0,1:T(2,128)(2,1)S(1)}, bf16[8,2]{0,1:T(2,128)(2,1)S(1)}, u32[]{:S(2)}, u32[]{:S(2)}) collective-permute-start(bf16[8,2]{0,1:T(2,128)(2,1)S(1)} %collective-permute-done.12), channel_id=1, source_target_pairs={{0,15},{1,0},{2,1},{3,2},{4,3},{5,4},{6,5},{7,6},{8,7},{9,8},{10,9... | collective-permute-start | bytes 104 | tf_op jit(solution)/shard_map/ppermute | solution.py:23
  214.7 1.3 collective-permute-done.13
  216.0 4.4 %collective-permute-start.14 = (bf16[8,2]{0,1:T(2,128)(2,1)S(1)}, bf16[8,2]{0,1:T(2,128)(2,1)S(1)}, u32[]{:S(2)}, u32[]{:S(2)}) collective-permute-start(bf16[8,2]{0,1:T(2,128)(2,1)S(1)} %collective-permute-done.13), channel_id=1, source_target_pairs={{0,15},{1,0},{2,1},{3,2},{4,3},{5,4},{6,5},{7,6},{8,7},{9,8},{10,9... | collective-permute-start | bytes 104 | tf_op jit(solution)/shard_map/ppermute | solution.py:23
  220.3 5.7 %collective-permute-done.6 = bf16[8,2]{0,1:T(2,128)(2,1)S(1)} collective-permute-done((bf16[8,2]{0,1:T(2,128)(2,1)S(1)}, bf16[8,2]{0,1:T(2,128)(2,1)S(1)}, u32[]{:S(2)}, u32[]{:S(2)}) %collective-permute-start.6) | collective-permute-done | bytes 64 | tf_op jit(solution)/shard_map/ppermute | solution.py:21
  226.0 5.7 %collective-permute-done.7 = bf16[8,2]{0,1:T(2,128)(2,1)S(1)} collective-permute-done((bf16[8,2]{0,1:T(2,128)(2,1)S(1)}, bf16[8,2]{0,1:T(2,128)(2,1)S(1)}, u32[]{:S(2)}, u32[]{:S(2)}) %collective-permute-start.7) | collective-permute-done | bytes 64 | tf_op jit(solution)/shard_map/ppermute | solution.py:21
  231.7 0.1 concatenate.26
  231.8 0.1 constant_dynamic-slice_fusion
  231.9 0.1 reshape.165
  232.0 0.6 gather_fusion.1
  232.6 0.1 copy.32
  232.7 0.1 copy.33
  232.8 0.1 maximum_divide_fusion.1
  232.9 0.1 div.25
  233.0 3.6 %fusion.22 = f32[640,401]{0,1:T(8,128)} fusion(f32[640,595]{1,0:T(8,128)S(1)} %bitcast.50, f32[640,595]{1,0:T(8,128)S(1)} %bitcast.49, f32[640]{0:T(1024)S(1)} %div.25, bf16[595,401]{1,0:T(8,128)(2,1)} %get-tuple-element.110, bf16[595,401]{1,0:T(8,128)(2,1)} %get-tuple-element.109), kind=kOutput, calls=%fused_computation.33 | convolution fusion | flops 615253376 | bytes 5029900 | tf_op jit(solution)/shard_map/dot_general | solution.py:94
  236.6 1.7 copy.35
  238.3 1.4 add.154
  (51 shorter events, 0.5 us)
Async XLA Ops:
  0.8 190.5 %collective-permute-start.8 = (bf16[8,2]{0,1:T(2,128)(2,1)S(1)}, bf16[8,2]{0,1:T(2,128)(2,1)S(1)}, u32[]{:S(2)}, u32[]{:S(2)}) collective-permute-start(bf16[8,2]{0,1:T(2,128)(2,1)S(1)} %get-tuple-element.113), channel_id=1, source_target_pairs={{0,15},{1,0},{2,1},{3,2},{4,3},{5,4},{6,5},{7,6},{8,7},{9,8},{10,9... | collective-permute-start | bytes 104 | tf_op jit(solution)/shard_map/ppermute | solution.py:23
  6.2 185.8 %collective-permute-start = (bf16[8,2]{0,1:T(2,128)(2,1)S(1)}, bf16[8,2]{0,1:T(2,128)(2,1)S(1)}, u32[]{:S(2)}, u32[]{:S(2)}) collective-permute-start(bf16[8,2]{0,1:T(2,128)(2,1)S(1)} %get-tuple-element.113), channel_id=1, source_target_pairs={{0,1},{1,2},{2,3},{3,4},{4,5},{5,6},{6,7},{7,8},{8,9},{9,10},{10,1... | collective-permute-start | bytes 104 | tf_op jit(solution)/shard_map/ppermute | solution.py:21
  191.2 2.1 collective-permute-start.9
  192.0 5.7 %collective-permute-start.1 = (bf16[8,2]{0,1:T(2,128)(2,1)S(1)}, bf16[8,2]{0,1:T(2,128)(2,1)S(1)}, u32[]{:S(2)}, u32[]{:S(2)}) collective-permute-start(bf16[8,2]{0,1:T(2,128)(2,1)S(1)} %collective-permute-done), channel_id=1, source_target_pairs={{0,1},{1,2},{2,3},{3,4},{4,5},{5,6},{6,7},{7,8},{8,9},{9,10},{10,1... | collective-permute-start | bytes 104 | tf_op jit(solution)/shard_map/ppermute | solution.py:21
  193.3 5.7 %collective-permute-start.10 = (bf16[8,2]{0,1:T(2,128)(2,1)S(1)}, bf16[8,2]{0,1:T(2,128)(2,1)S(1)}, u32[]{:S(2)}, u32[]{:S(2)}) collective-permute-start(bf16[8,2]{0,1:T(2,128)(2,1)S(1)} %collective-permute-done.9), channel_id=1, source_target_pairs={{0,15},{1,0},{2,1},{3,2},{4,3},{5,4},{6,5},{7,6},{8,7},{9,8},{10,9... | collective-permute-start | bytes 104 | tf_op jit(solution)/shard_map/ppermute | solution.py:23
  197.7 5.7 %collective-permute-start.2 = (bf16[8,2]{0,1:T(2,128)(2,1)S(1)}, bf16[8,2]{0,1:T(2,128)(2,1)S(1)}, u32[]{:S(2)}, u32[]{:S(2)}) collective-permute-start(bf16[8,2]{0,1:T(2,128)(2,1)S(1)} %collective-permute-done.1), channel_id=1, source_target_pairs={{0,1},{1,2},{2,3},{3,4},{4,5},{5,6},{6,7},{7,8},{8,9},{9,10},{10,1... | collective-permute-start | bytes 104 | tf_op jit(solution)/shard_map/ppermute | solution.py:21
  199.0 5.7 %collective-permute-start.11 = (bf16[8,2]{0,1:T(2,128)(2,1)S(1)}, bf16[8,2]{0,1:T(2,128)(2,1)S(1)}, u32[]{:S(2)}, u32[]{:S(2)}) collective-permute-start(bf16[8,2]{0,1:T(2,128)(2,1)S(1)} %collective-permute-done.10), channel_id=1, source_target_pairs={{0,15},{1,0},{2,1},{3,2},{4,3},{5,4},{6,5},{7,6},{8,7},{9,8},{10,9... | collective-permute-start | bytes 104 | tf_op jit(solution)/shard_map/ppermute | solution.py:23
  203.3 5.7 %collective-permute-start.3 = (bf16[8,2]{0,1:T(2,128)(2,1)S(1)}, bf16[8,2]{0,1:T(2,128)(2,1)S(1)}, u32[]{:S(2)}, u32[]{:S(2)}) collective-permute-start(bf16[8,2]{0,1:T(2,128)(2,1)S(1)} %collective-permute-done.2), channel_id=1, source_target_pairs={{0,1},{1,2},{2,3},{3,4},{4,5},{5,6},{6,7},{7,8},{8,9},{9,10},{10,1... | collective-permute-start | bytes 104 | tf_op jit(solution)/shard_map/ppermute | solution.py:21
  204.6 5.7 %collective-permute-start.12 = (bf16[8,2]{0,1:T(2,128)(2,1)S(1)}, bf16[8,2]{0,1:T(2,128)(2,1)S(1)}, u32[]{:S(2)}, u32[]{:S(2)}) collective-permute-start(bf16[8,2]{0,1:T(2,128)(2,1)S(1)} %collective-permute-done.11), channel_id=1, source_target_pairs={{0,15},{1,0},{2,1},{3,2},{4,3},{5,4},{6,5},{7,6},{8,7},{9,8},{10,9... | collective-permute-start | bytes 104 | tf_op jit(solution)/shard_map/ppermute | solution.py:23
  209.0 5.7 %collective-permute-start.4 = (bf16[8,2]{0,1:T(2,128)(2,1)S(1)}, bf16[8,2]{0,1:T(2,128)(2,1)S(1)}, u32[]{:S(2)}, u32[]{:S(2)}) collective-permute-start(bf16[8,2]{0,1:T(2,128)(2,1)S(1)} %collective-permute-done.3), channel_id=1, source_target_pairs={{0,1},{1,2},{2,3},{3,4},{4,5},{5,6},{6,7},{7,8},{8,9},{9,10},{10,1... | collective-permute-start | bytes 104 | tf_op jit(solution)/shard_map/ppermute | solution.py:21
  210.3 5.7 %collective-permute-start.13 = (bf16[8,2]{0,1:T(2,128)(2,1)S(1)}, bf16[8,2]{0,1:T(2,128)(2,1)S(1)}, u32[]{:S(2)}, u32[]{:S(2)}) collective-permute-start(bf16[8,2]{0,1:T(2,128)(2,1)S(1)} %collective-permute-done.12), channel_id=1, source_target_pairs={{0,15},{1,0},{2,1},{3,2},{4,3},{5,4},{6,5},{7,6},{8,7},{9,8},{10,9... | collective-permute-start | bytes 104 | tf_op jit(solution)/shard_map/ppermute | solution.py:23
  214.7 5.7 %collective-permute-start.5 = (bf16[8,2]{0,1:T(2,128)(2,1)S(1)}, bf16[8,2]{0,1:T(2,128)(2,1)S(1)}, u32[]{:S(2)}, u32[]{:S(2)}) collective-permute-start(bf16[8,2]{0,1:T(2,128)(2,1)S(1)} %collective-permute-done.4), channel_id=1, source_target_pairs={{0,1},{1,2},{2,3},{3,4},{4,5},{5,6},{6,7},{7,8},{8,9},{9,10},{10,1... | collective-permute-start | bytes 104 | tf_op jit(solution)/shard_map/ppermute | solution.py:21
  216.0 10.0 %collective-permute-start.14 = (bf16[8,2]{0,1:T(2,128)(2,1)S(1)}, bf16[8,2]{0,1:T(2,128)(2,1)S(1)}, u32[]{:S(2)}, u32[]{:S(2)}) collective-permute-start(bf16[8,2]{0,1:T(2,128)(2,1)S(1)} %collective-permute-done.13), channel_id=1, source_target_pairs={{0,15},{1,0},{2,1},{3,2},{4,3},{5,4},{6,5},{7,6},{8,7},{9,8},{10,9... | collective-permute-start | bytes 104 | tf_op jit(solution)/shard_map/ppermute | solution.py:23
  220.3 5.7 %collective-permute-start.6 = (bf16[8,2]{0,1:T(2,128)(2,1)S(1)}, bf16[8,2]{0,1:T(2,128)(2,1)S(1)}, u32[]{:S(2)}, u32[]{:S(2)}) collective-permute-start(bf16[8,2]{0,1:T(2,128)(2,1)S(1)} %collective-permute-done.5), channel_id=1, source_target_pairs={{0,1},{1,2},{2,3},{3,4},{4,5},{5,6},{6,7},{7,8},{8,9},{9,10},{10,1... | collective-permute-start | bytes 104 | tf_op jit(solution)/shard_map/ppermute | solution.py:21
  226.0 5.7 %collective-permute-start.7 = (bf16[8,2]{0,1:T(2,128)(2,1)S(1)}, bf16[8,2]{0,1:T(2,128)(2,1)S(1)}, u32[]{:S(2)}, u32[]{:S(2)}) collective-permute-start(bf16[8,2]{0,1:T(2,128)(2,1)S(1)} %collective-permute-done.6), channel_id=1, source_target_pairs={{0,1},{1,2},{2,3},{3,4},{4,5},{5,6},{6,7},{7,8},{8,9},{9,10},{10,1... | collective-permute-start | bytes 104 | tf_op jit(solution)/shard_map/ppermute | solution.py:21
  236.6 1.7 copy-start
